TPU v7x, 32 devices: a whole 2x2x4 slice. The times are simulated.
32 devices in a mesh: gx: 4 (over z), gy: 8 (over y, x, core).
Axes of the slice: x: 2, y: 2, z: 4, core: 2. Of those that a mesh axis runs over, the one named last changes fastest.
Arguments:
- features: bfloat16 [256, 20480], P(None, ('gx', 'gy')), may hold values from 0 to 1.5
- w_first: bfloat16 [20480, 256], P(('gx', 'gy')), may hold values from -0.078125 to 0.078125
- w_label: bfloat16 [256, 90112], P(None, ('gx', 'gy')), may hold values from -42 to 42
- label_ids: int32 [256, 8], replicated, may hold values from 0 to 90111, as said below
- label_count: int32 [256], replicated, may hold values from 1 to 8
Outputs:
- grad_first: bfloat16 [20480, 256], P(('gx', 'gy'))
- grad_label: bfloat16 [256, 90112], P(None, ('gx', 'gy'))
- mean_loss: float32 [], replicated
Inputs may be any that keep to these rules, and one draw needn't show every extreme that they name: `label_ids`: each document's 8 ids are distinct labels; slots at or past label_count are filled with ids that are ignored.
All inputs are finite; a program needn't handle non-finite values.
Results may differ from a plain program's by a relative error of at most 0.0085.
Values may be sent and summed in bfloat16 or wider, within the bound.
No kernel may reach another device: no remote copies, remote signals or barrier semaphores. Data moves between devices by JAX's collectives and lax.ppermute only.
A program may use at most 64 MiB of HBM per device.

v0:
```python
import jax
import jax.numpy as jnp
from jax import lax
from jax.sharding import PartitionSpec as P


def per_device(features, w_first, w_label, label_ids, label_count):
    partial_value = jnp.dot(features, w_first, preferred_element_type=jnp.float32)
    minor_share = lax.psum_scatter(partial_value, "gy", scatter_dimension=0, tiled=True)
    shares = lax.psum(minor_share, "gx")
    hidden = lax.all_gather(jnp.tanh(shares).astype(jnp.bfloat16), "gy", axis=0, tiled=True)
    logits = jnp.dot(hidden, w_label, preferred_element_type=jnp.float32)
    label_width = w_label.shape[1]
    offset = lax.axis_index(("gx", "gy")) * label_width
    local_ids = offset + lax.iota(jnp.int32, label_width)
    slot_total = label_ids.shape[1]
    in_count = lax.iota(jnp.int32, slot_total)[None, :] < label_count[:, None]
    matches = jnp.zeros(logits.shape, jnp.float32)
    for slot_index in range(slot_total):
        hit = in_count[:, slot_index : slot_index + 1] & (
            label_ids[:, slot_index : slot_index + 1] == local_ids[None, :]
        )
        matches = matches + jnp.where(hit, 1.0, 0.0)
    positive = jnp.sum(matches * logits, axis=1)
    local_max = jnp.max(logits, axis=1)
    row_max = lax.pmax(local_max, ("gx", "gy"))
    local_sum = jnp.sum(jnp.exp(logits - row_max[:, None]), axis=1)
    norm_sum, picked = lax.psum((local_sum, positive), ("gx", "gy"))
    lse = row_max + jnp.log(norm_sum)
    doc_count = label_count.astype(jnp.float32)
    mean_loss = jnp.mean(lse - picked / doc_count)
    grad_logits = (jnp.exp(logits - lse[:, None]) - matches / doc_count[:, None]).astype(
        jnp.bfloat16
    )
    grad_label = lax.dot_general(
        hidden, grad_logits, (((0,), (0,)), ((), ())), preferred_element_type=jnp.float32
    ).astype(jnp.bfloat16)
    grad_part = lax.dot_general(
        grad_logits, w_label, (((1,), (1,)), ((), ())), preferred_element_type=jnp.float32
    )
    grad_hidden = lax.psum(grad_part, ("gx", "gy"))
    hidden_wide = hidden.astype(jnp.float32)
    grad_inner = (grad_hidden * (1.0 - hidden_wide * hidden_wide)).astype(jnp.bfloat16)
    grad_first = lax.dot_general(
        features, grad_inner, (((0,), (0,)), ((), ())), preferred_element_type=jnp.float32
    ).astype(jnp.bfloat16)
    return (grad_first, grad_label, mean_loss)


def solution(mesh):
    placed = (P(None, ("gx", "gy")), P(("gx", "gy"), None), P(None, ("gx", "gy")), P(), P())
    return jax.shard_map(
        per_device,
        mesh=mesh,
        in_specs=placed,
        out_specs=(P(("gx", "gy"), None), P(None, ("gx", "gy")), P()),
        check_vma=False,
    )
```

profile of v0, /device:TPU:0, one launch (start us, length us, event | category | flops | bytes accessed | tf_op | source)
XLA Modules:
  0.0 310.3 jit_solution(5411630395774496116)
XLA Ops:
  7.2 0.0 copy-start
  7.2 0.0 reduce-scatter.2.cloned.1.call-start
  7.2 2.1 fusion.5
  9.4 0.0 reduce-scatter.2.cloned.1.call-update
  9.4 0.0 all-reduce.3.cloned.1.call-start
  9.5 0.7 iota_compare_fusion
  10.1 0.7 convert_element_type.25
  10.9 1.0 fusion.3
  11.9 36.2 %reduce-scatter.2.cloned.1.call-done = f32[32,256]{1,0:T(8,128)} async-done(((f32[256,256]{1,0:T(8,128)}), f32[32,256]{1,0:T(8,128)}) %reduce-scatter.2.cloned.1.call-update) | async-done | bytes 32784 | tf_op jit(solution)/shard_map/reduce_scatter | solution.py:9
  48.0 19.6 %psum.28 = f32[32,256]{1,0:T(8,128)S(1)} all-reduce(f32[32,256]{1,0:T(8,128)} %reduce-scatter.2.cloned.1.call-done), channel_id=1, replica_groups=mesh['gx'=4,'gy'=8] {'gx'}, use_global_device_ids=true, to_apply=%region_1.0 | all-reduce | flops 8192 | bytes 65536 | tf_op jit(solution)/shard_map/psum | solution.py:10
  67.6 9.2 %all_gather.3 = bf16[256,256]{1,0:T(8,128)(2,1)S(1)} all-gather(bf16[32,256]{1,0:T(8,128)(2,1)S(1)} %tanh_convert_fusion), channel_id=1, replica_groups=mesh['gx'=4,'gy'=8] {'gy'}, dimensions={0}, use_global_device_ids=true | all-gather | bytes 147456 | tf_op jit(solution)/shard_map/all_gather | solution.py:11
  76.8 2.1 fusion.4
  78.9 37.4 %pmax.7 = f32[256]{0:T(256)S(1)} all-reduce(f32[256]{0:T(256)S(1)} %get-tuple-element.31), channel_id=1, replica_groups=mesh['gx'=4,'gy'=8] {'gx','gy'}, use_global_device_ids=true, to_apply=%region_3.4 | all-reduce | flops 256 | bytes 2048 | tf_op jit(solution)/shard_map/pmax | solution.py:26
  116.3 6.8 %multiply_reduce_fusion = (f32[256]{0:T(256)S(1)}, f32[256]{0:T(256)S(1)}) fusion(f32[256,2816]{1,0:T(8,128)} %get-tuple-element.32, s32[256]{0:T(256)S(1)} %bitcast.31, pred[256]{0:T(512)(128)(4,1)S(1)} %get-tuple-element.12, s32[256]{0:T(256)S(1)} %bitcast.33, pred[256]{0:T(512)(128)(4,1)S(1)} %get-tuple-element.13, s32[256]{0:T(256)S(1)} %bitcast.21, ...), kind=kLoop, calls=%fused_computation.1 | loop fusion | flops 25230848 | bytes 2908160 | tf_op jit(solution)/shard_map/reduce_sum | solution.py:24
  123.1 40.8 %all-reduce = (f32[256]{0:T(256)S(1)}, f32[256]{0:T(256)S(1)}) all-reduce(f32[256]{0:T(256)S(1)} %get-tuple-element.10, f32[256]{0:T(256)S(1)} %get-tuple-element.9), channel_id=1, replica_groups=mesh['gx'=4,'gy'=8] {'gx','gy'}, use_global_device_ids=true, to_apply=%region_5.6 | all-reduce | flops 512 | bytes 4096 | tf_op jit(solution)/shard_map/psum | solution.py:28
  164.0 0.6 subtract_reduce_fusion
  164.6 7.5 %subtract_convert_fusion = bf16[256,2816]{1,0:T(8,128)(2,1)S(1)} fusion(f32[256,2816]{1,0:T(8,128)} %get-tuple-element.32, f32[256]{0:T(256)S(1)} %convert_element_type.25, f32[256]{0:T(256)S(1)} %get-tuple-element.22, s32[256]{0:T(256)S(1)} %bitcast.32, pred[256]{0:T(512)(128)(4,1)S(1)} %get-tuple-element.12, s32[256]{0:T(256)S(1)} %bitcast.34, ...), kind=kLoop, calls=%fused_computation.2 | loop fusion | flops 25231360 | bytes 4348928 | tf_op jit(solution)/shard_map/convert_element_type | solution.py:32
  172.1 0.0 copy-start.1
  172.1 1.3 fusion.6
  173.4 0.0 all-reduce.3.cloned.1.call-update
  173.4 1.7 convolution_convert_fusion
  175.8 124.4 %all-reduce.3.cloned.1.call-done = f32[256,256]{1,0:T(8,128)} async-done(((f32[256,256]{1,0:T(8,128)}), f32[256,256]{1,0:T(8,128)}) %all-reduce.3.cloned.1.call-update) | async-done | bytes 262160 | tf_op jit(solution)/shard_map/psum | solution.py:41
  300.2 1.2 fusion
  301.4 0.9 copy.9
  (7 shorter events, 0.1 us)
Async XLA Ops:
  7.2 69.6 %copy-start = (bf16[256,2816]{1,0:T(8,128)(2,1)S(1)}, bf16[256,2816]{1,0:T(8,128)(2,1)}, u32[]{:S(2)}) copy-start(bf16[256,2816]{1,0:T(8,128)(2,1)} %param.7) | copy-start | bytes 4325380
  7.2 40.8 %reduce-scatter.2.cloned.1.call-start = ((), (), s32[]{:S(2)}) async-start(), calls=%async_computation.1 | async-start | bytes 294912 | tf_op jit(solution)/shard_map/reduce_scatter | solution.py:9
  9.4 290.8 %all-reduce.3.cloned.1.call-start = ((), (), s32[]{:S(2)}) async-start(), calls=%async_computation.2 | async-start | bytes 524288 | tf_op jit(solution)/shard_map/psum | solution.py:41
  76.8 87.2 %copy-start.2 = (s32[256]{0:T(256)S(1)}, s32[256]{0:T(256)}, u32[]{:S(2)}) copy-start(s32[256]{0:T(256)} %param.9) | copy-start | bytes 3076
  172.1 128.1 %copy-start.1 = (bf16[256,640]{1,0:T(8,128)(2,1)S(1)}, bf16[256,640]{1,0:T(8,128)(2,1)}, u32[]{:S(2)}) copy-start(bf16[256,640]{1,0:T(8,128)(2,1)} %param.5) | copy-start | bytes 983044
Sparse Core Ops, SparseCore 0:
  11.6 36.3 reduce-scatter.1
  173.5 126.5 all-reduce.2
where the time goes:
time: 311 us; the launch traced here: 310 us
  waiting for transfers between devices  161 us (52%)
  blocking collectives  107 us (34%)
  other arithmetic  16.3 us (5%)
  between operations  15.9 us (5%)
  matrix products  8.48 us (3%)
    psum x1, waiting for transfers between devices, per_device(): grad_hidden = lax.psum(grad_part, ('gx', 'gy'))  124 us
    psum x1, blocking collectives, per_device(): norm_sum, picked = lax.psum((local_sum, positive), ('gx', 'gy'))  40.8 us
    pmax x1, blocking collectives, per_device(): row_max = lax.pmax(local_max, ('gx', 'gy'))  37.4 us
    reduce_scatter x1, waiting for transfers between devices, per_device(): lax.psum_scatter(partial_value, 'gy', scatter_dimension=0, tiled=True)  36.2 us
    psum x1, blocking collectives, per_device(): shares = lax.psum(minor_share, 'gx')  19.6 us
    all_gather x1, blocking collectives, per_device(): lax.all_gather(jnp.tanh(shares).astype(jnp.bfloat16), 'gy', axis=0, tiled...  9.17 us
    convert_element_type x1, other arithmetic, per_device(): (jnp.exp(logits - lse[:, None]) - matches / doc_count[:, None]).astype(jn...  7.53 us
    reduce_sum x1, other arithmetic, per_device(): positive = jnp.sum(matches * logits, axis=1)  6.79 us
  transfers between devices with their start and end apart: 2, of which 2 were waited for; matrix products, arithmetic and copies ran while one was open for 1% of the time, Pallas kernels for 0%

commit v1 on v0

--- a/solution.py
+++ b/solution.py
@@ -38,7 +38,7 @@
     grad_part = lax.dot_general(
         grad_logits, w_label, (((1,), (1,)), ((), ())), preferred_element_type=jnp.float32
     )
-    grad_hidden = lax.psum(grad_part, ("gx", "gy"))
+    grad_hidden = jnp.sum(lax.all_gather(grad_part, ("gx", "gy")), axis=0)
     hidden_wide = hidden.astype(jnp.float32)
     grad_inner = (grad_hidden * (1.0 - hidden_wide * hidden_wide)).astype(jnp.bfloat16)
     grad_first = lax.dot_general(

time: 311 us -> 264 us (0.85)
  waiting for transfers between devices: 161 us -> 111 us
  other arithmetic: 16.3 us -> 20.3 us
    psum x1 -> x0, waiting for transfers between devices: 124 us -> none  [per_device(): grad_hidden = lax.psum(grad_part, ('gx', 'gy'))]
    all_gather x0 -> x1, waiting for transfers between devices: none -> 74.8 us  [per_device(): grad_hidden = jnp.sum(lax.all_gather(grad_part, ('gx', 'gy')), axis=0)]
    reduce_sum x0 -> x1, other arithmetic: none -> 3.97 us  [per_device(): grad_hidden = jnp.sum(lax.all_gather(grad_part, ('gx', 'gy')), axis=0)]
  transfers between devices with their start and end apart: 2 -> 2, of which waited for: 2 -> 2; matrix products, arithmetic and copies ran while one was open for 1% -> 2% of each run, Pallas kernels for 0% -> 0%
where the time goes in v1:
time: 264 us
  waiting for transfers between devices  111 us (42%)
  blocking collectives  107 us (41%)
  other arithmetic  20.3 us (8%)
  between operations  15.9 us (6%)
  matrix products  7.55 us (3%)
    all_gather x1, waiting for transfers between devices, per_device(): grad_hidden = jnp.sum(lax.all_gather(grad_part, ('gx', 'gy')), axis=0)  74.8 us
    psum x1, blocking collectives, per_device(): norm_sum, picked = lax.psum((local_sum, positive), ('gx', 'gy'))  40.8 us
    pmax x1, blocking collectives, per_device(): row_max = lax.pmax(local_max, ('gx', 'gy'))  37.4 us
    reduce_scatter x1, waiting for transfers between devices, per_device(): lax.psum_scatter(partial_value, 'gy', scatter_dimension=0, tiled=True)  36.2 us
    psum x1, blocking collectives, per_device(): shares = lax.psum(minor_share, 'gx')  19.6 us
    all_gather x1, blocking collectives, per_device(): lax.all_gather(jnp.tanh(shares).astype(jnp.bfloat16), 'gy', axis=0, tiled...  9.17 us
    convert_element_type x1, other arithmetic, per_device(): (jnp.exp(logits - lse[:, None]) - matches / doc_count[:, None]).astype(jn...  7.53 us
    reduce_sum x1, other arithmetic, per_device(): positive = jnp.sum(matches * logits, axis=1)  6.79 us
  transfers between devices with their start and end apart: 2, of which 2 were waited for; matrix products, arithmetic and copies ran while one was open for 2% of the time, Pallas kernels for 0%

profile of v1, /device:TPU:0, one launch (start us, length us, event | category | flops | bytes accessed | tf_op | source)
XLA Modules:
  0.0 263.7 jit_solution(5460447911230874729)
XLA Ops:
  7.2 0.0 copy-start
  7.2 0.0 reduce-scatter.2.cloned.1.call-start
  7.2 2.1 fusion.5
  9.4 0.0 reduce-scatter.2.cloned.1.call-update
  9.4 0.0 all-gather.3.cloned.1.call-start
  9.5 0.7 iota_compare_fusion
  10.1 0.7 convert_element_type.25
  10.9 1.0 fusion.3
  11.9 36.2 %reduce-scatter.2.cloned.1.call-done = f32[32,256]{1,0:T(8,128)} async-done(((f32[256,256]{1,0:T(8,128)}), f32[32,256]{1,0:T(8,128)}) %reduce-scatter.2.cloned.1.call-update) | async-done | bytes 32784 | tf_op jit(solution)/shard_map/reduce_scatter | solution.py:9
  48.0 19.6 %psum.21 = f32[32,256]{1,0:T(8,128)S(1)} all-reduce(f32[32,256]{1,0:T(8,128)} %reduce-scatter.2.cloned.1.call-done), channel_id=1, replica_groups=mesh['gx'=4,'gy'=8] {'gx'}, use_global_device_ids=true, to_apply=%region_1.0 | all-reduce | flops 8192 | bytes 65536 | tf_op jit(solution)/shard_map/psum | solution.py:10
  67.6 9.2 %all_gather.9 = bf16[256,256]{1,0:T(8,128)(2,1)S(1)} all-gather(bf16[32,256]{1,0:T(8,128)(2,1)S(1)} %tanh_convert_fusion), channel_id=1, replica_groups=mesh['gx'=4,'gy'=8] {'gy'}, dimensions={0}, use_global_device_ids=true | all-gather | bytes 147456 | tf_op jit(solution)/shard_map/all_gather | solution.py:11
  76.8 2.1 fusion.4
  78.9 37.4 %pmax.7 = f32[256]{0:T(256)S(1)} all-reduce(f32[256]{0:T(256)S(1)} %get-tuple-element.31), channel_id=1, replica_groups=mesh['gx'=4,'gy'=8] {'gx','gy'}, use_global_device_ids=true, to_apply=%region_3.4 | all-reduce | flops 256 | bytes 2048 | tf_op jit(solution)/shard_map/pmax | solution.py:26
  116.3 6.8 %multiply_reduce_fusion = (f32[256]{0:T(256)S(1)}, f32[256]{0:T(256)S(1)}) fusion(f32[256,2816]{1,0:T(8,128)} %get-tuple-element.32, s32[256]{0:T(256)S(1)} %bitcast.33, pred[256]{0:T(512)(128)(4,1)S(1)} %get-tuple-element.12, s32[256]{0:T(256)S(1)} %bitcast.35, pred[256]{0:T(512)(128)(4,1)S(1)} %get-tuple-element.13, s32[256]{0:T(256)S(1)} %bitcast.23, ...), kind=kLoop, calls=%fused_computation.1 | loop fusion | flops 25230848 | bytes 2908160 | tf_op jit(solution)/shard_map/reduce_sum | solution.py:24
  123.1 40.8 %all-reduce = (f32[256]{0:T(256)S(1)}, f32[256]{0:T(256)S(1)}) all-reduce(f32[256]{0:T(256)S(1)} %get-tuple-element.10, f32[256]{0:T(256)S(1)} %get-tuple-element.9), channel_id=1, replica_groups=mesh['gx'=4,'gy'=8] {'gx','gy'}, use_global_device_ids=true, to_apply=%region_5.6 | all-reduce | flops 512 | bytes 4096 | tf_op jit(solution)/shard_map/psum | solution.py:28
  164.0 0.6 subtract_reduce_fusion
  164.6 7.5 %subtract_convert_fusion = bf16[256,2816]{1,0:T(8,128)(2,1)S(1)} fusion(f32[256,2816]{1,0:T(8,128)} %get-tuple-element.32, f32[256]{0:T(256)S(1)} %convert_element_type.25, f32[256]{0:T(256)S(1)} %get-tuple-element.22, s32[256]{0:T(256)S(1)} %bitcast.34, pred[256]{0:T(512)(128)(4,1)S(1)} %get-tuple-element.12, s32[256]{0:T(256)S(1)} %bitcast.36, ...), kind=kLoop, calls=%fused_computation.2 | loop fusion | flops 25231360 | bytes 4348928 | tf_op jit(solution)/shard_map/convert_element_type | solution.py:32
  172.1 1.3 fusion.6
  173.4 0.0 all-gather.3.cloned.1.call-update
  174.1 1.7 convolution_convert_fusion
  175.8 74.8 %all-gather.3.cloned.1.call-done = f32[8192,256]{1,0:T(8,128)} async-done(((f32[256,256]{1,0:T(8,128)}), f32[8192,256]{1,0:T(8,128)}) %all-gather.3.cloned.1.call-update) | async-done | bytes 8388624 | tf_op jit(solution)/shard_map/all_gather | solution.py:41
  250.6 4.0 %reduce_sum.37 = f32[256,256]{1,0:T(8,128)S(1)} reduce(f32[32,256,256]{2,1,0:T(8,128)} %bitcast.20, f32[]{:T(128)} %constant.9.clone.1), dimensions={0}, to_apply=%region_6.7 | reduce | flops 2031616 | bytes 8650756 | tf_op jit(solution)/shard_map/reduce_sum | solution.py:41
  254.5 0.3 fusion
  254.8 0.9 copy.9
  (8 shorter events, 0.1 us)
Async XLA Ops:
  7.2 69.6 %copy-start = (bf16[256,2816]{1,0:T(8,128)(2,1)S(1)}, bf16[256,2816]{1,0:T(8,128)(2,1)}, u32[]{:S(2)}) copy-start(bf16[256,2816]{1,0:T(8,128)(2,1)} %param.7) | copy-start | bytes 4325380
  7.2 40.8 %reduce-scatter.2.cloned.1.call-start = ((), (), s32[]{:S(2)}) async-start(), calls=%async_computation.1 | async-start | bytes 294912 | tf_op jit(solution)/shard_map/reduce_scatter | solution.py:9
  9.4 241.2 %all-gather.3.cloned.1.call-start = ((), (), s32[]{:S(2)}) async-start(), calls=%async_computation.2 | async-start | bytes 8650752 | tf_op jit(solution)/shard_map/all_gather | solution.py:41
  76.8 87.2 %copy-start.2 = (s32[256]{0:T(256)S(1)}, s32[256]{0:T(256)}, u32[]{:S(2)}) copy-start(s32[256]{0:T(256)} %param.9) | copy-start | bytes 3076
  250.6 4.0 %copy-start.1 = (bf16[256,640]{1,0:T(8,128)(2,1)S(1)}, bf16[256,640]{1,0:T(8,128)(2,1)}, u32[]{:S(2)}) copy-start(bf16[256,640]{1,0:T(8,128)(2,1)} %param.5) | copy-start | bytes 983044
Sparse Core Ops, SparseCore 0:
  11.6 36.3 reduce-scatter.1
  173.6 76.9 all-gather.2

commit v2 on v0

--- a/solution.py
+++ b/solution.py
@@ -25,7 +25,7 @@
     local_max = jnp.max(logits, axis=1)
     row_max = lax.pmax(local_max, ("gx", "gy"))
     local_sum = jnp.sum(jnp.exp(logits - row_max[:, None]), axis=1)
-    norm_sum, picked = lax.psum((local_sum, positive), ("gx", "gy"))
+    norm_sum, picked = lax.psum(lax.psum((local_sum, positive), "gy"), "gx")
     lse = row_max + jnp.log(norm_sum)
     doc_count = label_count.astype(jnp.float32)
     mean_loss = jnp.mean(lse - picked / doc_count)

time: 311 us -> 291 us (0.936)
  blocking collectives: 107 us -> 89.5 us
    psum x1 -> x2, blocking collectives: 40.8 us -> 23.4 us  [per_device(): norm_sum, picked = lax.psum(lax.psum((local_sum, positive), 'gy'), 'gx')]
where the time goes in v2:
time: 291 us; the launch traced here: 290 us
  waiting for transfers between devices  158 us (54%)
  blocking collectives  89.5 us (31%)
  other arithmetic  16.3 us (6%)
  between operations  15.9 us (5%)
  matrix products  8.49 us (3%)
    psum x1, waiting for transfers between devices, per_device(): grad_hidden = lax.psum(grad_part, ('gx', 'gy'))  122 us
    pmax x1, blocking collectives, per_device(): row_max = lax.pmax(local_max, ('gx', 'gy'))  37.4 us
    reduce_scatter x1, waiting for transfers between devices, per_device(): lax.psum_scatter(partial_value, 'gy', scatter_dimension=0, tiled=True)  36.2 us
    psum x2, blocking collectives, per_device(): norm_sum, picked = lax.psum(lax.psum((local_sum, positive), 'gy'), 'gx')  23.4 us
    psum x1, blocking collectives, per_device(): shares = lax.psum(minor_share, 'gx')  19.6 us
    all_gather x1, blocking collectives, per_device(): lax.all_gather(jnp.tanh(shares).astype(jnp.bfloat16), 'gy', axis=0, tiled...  9.17 us
    convert_element_type x1, other arithmetic, per_device(): (jnp.exp(logits - lse[:, None]) - matches / doc_count[:, None]).astype(jn...  7.53 us
    reduce_sum x1, other arithmetic, per_device(): positive = jnp.sum(matches * logits, axis=1)  6.79 us
  transfers between devices with their start and end apart: 2, of which 2 were waited for; matrix products, arithmetic and copies ran while one was open for 1% of the time, Pallas kernels for 0%

profile of v2, /device:TPU:0, one launch (start us, length us, event | category | flops | bytes accessed | tf_op | source)
XLA Modules:
  0.0 290.1 jit_solution(493678034055656992)
XLA Ops:
  7.2 0.0 copy-start
  7.2 0.0 reduce-scatter.2.cloned.1.call-start
  7.2 2.1 fusion.5
  9.4 0.0 reduce-scatter.2.cloned.1.call-update
  9.4 0.0 all-reduce.4.cloned.1.call-start
  9.5 0.7 iota_compare_fusion
  10.1 0.7 convert_element_type.25
  10.9 1.0 fusion.3
  11.9 36.2 %reduce-scatter.2.cloned.1.call-done = f32[32,256]{1,0:T(8,128)} async-done(((f32[256,256]{1,0:T(8,128)}), f32[32,256]{1,0:T(8,128)}) %reduce-scatter.2.cloned.1.call-update) | async-done | bytes 32784 | tf_op jit(solution)/shard_map/reduce_scatter | solution.py:9
  48.0 19.6 %psum.42 = f32[32,256]{1,0:T(8,128)S(1)} all-reduce(f32[32,256]{1,0:T(8,128)} %reduce-scatter.2.cloned.1.call-done), channel_id=1, replica_groups=mesh['gx'=4,'gy'=8] {'gx'}, use_global_device_ids=true, to_apply=%region_1.0 | all-reduce | flops 8192 | bytes 65536 | tf_op jit(solution)/shard_map/psum | solution.py:10
  67.6 9.2 %all_gather.3 = bf16[256,256]{1,0:T(8,128)(2,1)S(1)} all-gather(bf16[32,256]{1,0:T(8,128)(2,1)S(1)} %tanh_convert_fusion), channel_id=1, replica_groups=mesh['gx'=4,'gy'=8] {'gy'}, dimensions={0}, use_global_device_ids=true | all-gather | bytes 147456 | tf_op jit(solution)/shard_map/all_gather | solution.py:11
  76.8 2.1 fusion.4
  78.9 37.4 %pmax.7 = f32[256]{0:T(256)S(1)} all-reduce(f32[256]{0:T(256)S(1)} %get-tuple-element.33), channel_id=1, replica_groups=mesh['gx'=4,'gy'=8] {'gx','gy'}, use_global_device_ids=true, to_apply=%region_3.4 | all-reduce | flops 256 | bytes 2048 | tf_op jit(solution)/shard_map/pmax | solution.py:26
  116.3 6.8 %multiply_reduce_fusion = (f32[256]{0:T(256)S(1)}, f32[256]{0:T(256)S(1)}) fusion(f32[256,2816]{1,0:T(8,128)} %get-tuple-element.34, s32[256]{0:T(256)S(1)} %bitcast.31, pred[256]{0:T(512)(128)(4,1)S(1)} %get-tuple-element.12, s32[256]{0:T(256)S(1)} %bitcast.33, pred[256]{0:T(512)(128)(4,1)S(1)} %get-tuple-element.13, s32[256]{0:T(256)S(1)} %bitcast.21, ...), kind=kLoop, calls=%fused_computation.1 | loop fusion | flops 25230848 | bytes 2908160 | tf_op jit(solution)/shard_map/reduce_sum | solution.py:24
  123.1 12.7 %all-reduce = (f32[256]{0:T(256)S(1)}, f32[256]{0:T(256)S(1)}) all-reduce(f32[256]{0:T(256)S(1)} %get-tuple-element.10, f32[256]{0:T(256)S(1)} %get-tuple-element.9), channel_id=1, replica_groups=mesh['gx'=4,'gy'=8] {'gy'}, use_global_device_ids=true, to_apply=%region_5.6 | all-reduce | flops 512 | bytes 4096 | tf_op jit(solution)/shard_map/psum | solution.py:28
  135.8 10.7 %all-reduce.1 = (f32[256]{0:T(256)S(1)}, f32[256]{0:T(256)S(1)}) all-reduce(f32[256]{0:T(256)S(1)} %get-tuple-element.19, f32[256]{0:T(256)S(1)} %get-tuple-element.20), channel_id=1, replica_groups=mesh['gx'=4,'gy'=8] {'gx'}, use_global_device_ids=true, to_apply=%region_6.7 | all-reduce | flops 512 | bytes 4096 | tf_op jit(solution)/shard_map/psum | solution.py:28
  146.5 0.6 subtract_reduce_fusion
  147.1 7.5 %subtract_convert_fusion = bf16[256,2816]{1,0:T(8,128)(2,1)S(1)} fusion(f32[256,2816]{1,0:T(8,128)} %get-tuple-element.34, f32[256]{0:T(256)S(1)} %convert_element_type.25, f32[256]{0:T(256)S(1)} %get-tuple-element.24, s32[256]{0:T(256)S(1)} %bitcast.32, pred[256]{0:T(512)(128)(4,1)S(1)} %get-tuple-element.12, s32[256]{0:T(256)S(1)} %bitcast.34, ...), kind=kLoop, calls=%fused_computation.2 | loop fusion | flops 25231360 | bytes 4348928 | tf_op jit(solution)/shard_map/convert_element_type | solution.py:32
  154.6 1.3 fusion.6
  155.9 0.0 all-reduce.4.cloned.1.call-update
  155.9 1.7 convolution_convert_fusion
  158.3 121.7 %all-reduce.4.cloned.1.call-done = f32[256,256]{1,0:T(8,128)} async-done(((f32[256,256]{1,0:T(8,128)}), f32[256,256]{1,0:T(8,128)}) %all-reduce.4.cloned.1.call-update) | async-done | bytes 262160 | tf_op jit(solution)/shard_map/psum | solution.py:41
  280.0 1.3 fusion
  281.2 0.9 copy.9
  (8 shorter events, 0.1 us)
Async XLA Ops:
  7.2 69.6 %copy-start = (bf16[256,2816]{1,0:T(8,128)(2,1)S(1)}, bf16[256,2816]{1,0:T(8,128)(2,1)}, u32[]{:S(2)}) copy-start(bf16[256,2816]{1,0:T(8,128)(2,1)} %param.7) | copy-start | bytes 4325380
  7.2 40.8 %reduce-scatter.2.cloned.1.call-start = ((), (), s32[]{:S(2)}) async-start(), calls=%async_computation.1 | async-start | bytes 294912 | tf_op jit(solution)/shard_map/reduce_scatter | solution.py:9
  9.4 270.6 %all-reduce.4.cloned.1.call-start = ((), (), s32[]{:S(2)}) async-start(), calls=%async_computation.2 | async-start | bytes 524288 | tf_op jit(solution)/shard_map/psum | solution.py:41
  76.8 69.7 %copy-start.2 = (s32[256]{0:T(256)S(1)}, s32[256]{0:T(256)}, u32[]{:S(2)}) copy-start(s32[256]{0:T(256)} %param.9) | copy-start | bytes 3076
  154.6 125.3 %copy-start.1 = (bf16[256,640]{1,0:T(8,128)(2,1)S(1)}, bf16[256,640]{1,0:T(8,128)(2,1)}, u32[]{:S(2)}) copy-start(bf16[256,640]{1,0:T(8,128)(2,1)} %param.5) | copy-start | bytes 983044
Sparse Core Ops, SparseCore 0:
  11.6 36.3 reduce-scatter.1
  156.1 123.8 all-reduce.3
